TPU v7x, 512 devices: a whole 4x4x16 slice. The times are simulated.
512 devices in a mesh: dp: 128 (over y, z, core), mp: 4 (over x).
Axes of the slice: x: 4, y: 4, z: 16, core: 2. Of those that a mesh axis runs over, the one named last changes fastest.
Arguments:
- embeddings: bfloat16 [32768, 768], P('dp'), may hold values from -8192 to 8192
- cluster_ids: int32 [32768], P('dp'), may hold values from 0 to 511, as said below
Outputs:
- scores: float32 [32768], P('dp')
Inputs may be any that keep to these rules, and one draw needn't show every extreme that they name: `cluster_ids`: the owner of cluster c is the index c // 4 of dp. Of the 256 rows of one index of dp, at most 4 lie in the clusters of one owner, and some owner gets exactly 4 rows from every index of dp.
All inputs are finite; a program needn't handle non-finite values.
Results may differ from a plain program's by a relative error of at most 0.0018.
Values may be sent and summed in bfloat16 or wider, within the bound.
A program may use at most 64 MiB of HBM per device.

v0:
```python
import jax
import jax.numpy as jnp
from jax import lax
from jax.sharding import PartitionSpec as P

CPO = 4


def contract_rows(left_rows, right_rows):
    return lax.dot_general(
        left_rows, right_rows, (((0,), (0,)), ((), ())), preferred_element_type=jnp.float32
    )


def normalize_rows(values):
    widened = values.astype(jnp.float32)
    square_sum = jnp.sum(widened * widened, axis=1, keepdims=True)
    inverse_norm = lax.rsqrt(square_sum + 1e-06)
    return (widened * inverse_norm).astype(jnp.bfloat16)


def best_match(queries, query_ids, query_start, key_units, key_ids):
    similarity = lax.dot_general(
        queries, key_units, (((1,), (1,)), ((), ())), preferred_element_type=jnp.float32
    )
    query_pos = query_start + jnp.arange(queries.shape[0], dtype=jnp.int32)
    key_pos = jnp.arange(key_units.shape[0], dtype=jnp.int32)
    same_cluster = (
        (query_ids[:, None] == key_ids[None, :])
        & (query_ids[:, None] >= 0)
        & (query_pos[:, None] != key_pos[None, :])
    )
    return jnp.max(jnp.where(same_cluster, similarity, -1.0), axis=1)


def local(embeddings, cluster_ids):
    row_count, feat_width = embeddings.shape
    dp_count = lax.axis_size("dp")
    mp_count = lax.axis_size("mp")
    mp_index = lax.axis_index("mp")
    pair_cap = 2 * row_count // dp_count
    slot_count = dp_count * pair_cap
    quarter_len = slot_count // mp_count
    identity = jnp.eye(feat_width, dtype=jnp.float32)
    row_share = row_count // mp_count
    own_rows = lax.dynamic_slice_in_dim(embeddings, mp_index * row_share, row_share, 0)
    moments = lax.psum(contract_rows(own_rows, own_rows), ("dp", "mp"))
    chol_factor = jnp.linalg.cholesky(moments / float(row_count * dp_count) + 0.001 * identity)
    whitening = jax.scipy.linalg.solve_triangular(chol_factor, identity, lower=True).astype(
        jnp.bfloat16
    )
    owner_ids = cluster_ids // CPO
    owner_hits = (owner_ids[:, None] == jnp.arange(dp_count, dtype=jnp.int32)[None, :]).astype(
        jnp.int32
    )
    earlier_hits = jnp.cumsum(owner_hits, axis=0) - owner_hits
    row_rank = jnp.sum(earlier_hits * owner_hits, axis=1)
    col_share = feat_width // mp_count
    whiten_part = lax.dynamic_slice_in_dim(whitening, mp_index * col_share, col_share, 0)
    whitened = lax.dot_general(
        embeddings, whiten_part, (((1,), (1,)), ((), ())), preferred_element_type=jnp.float32
    ).astype(jnp.bfloat16)
    slot_index = owner_ids * pair_cap + row_rank
    send_rows = jnp.zeros((slot_count, col_share), jnp.bfloat16).at[slot_index].set(whitened)
    send_ids = jnp.full((slot_count,), -1, jnp.int32).at[slot_index].set(cluster_ids)
    got_rows, got_ids = (
        lax.all_to_all(send_rows, "dp", split_axis=0, concat_axis=0, tiled=True),
        lax.all_to_all(send_ids, "dp", split_axis=0, concat_axis=0, tiled=True),
    )
    key_rows = lax.all_gather(got_rows, "mp", axis=1, tiled=True)
    unit = normalize_rows(key_rows)
    query_start = mp_index * quarter_len
    queries = lax.dynamic_slice_in_dim(unit, query_start, quarter_len, 0)
    query_ids = lax.dynamic_slice_in_dim(got_ids, query_start, quarter_len, 0)
    best_score = best_match(queries, query_ids, query_start, unit, got_ids)
    all_scores = lax.all_gather(best_score, "mp", axis=0, tiled=True)
    returned = lax.all_to_all(all_scores, "dp", split_axis=0, concat_axis=0, tiled=True)
    return returned[slot_index]


def solution(mesh):
    in_specs = (P("dp", None), P("dp"))
    out_specs = P("dp")
    return jax.shard_map(local, mesh=mesh, in_specs=in_specs, out_specs=out_specs, check_vma=False)
```

profile of v0, /device:TPU:1, one launch (start us, length us, event | category | flops | bytes accessed | tf_op | source)
XLA Modules:
  0.0 857.0 jit_solution(18049372178460269238)
XLA Ops:
  7.5 2.0 fusion.53
  10.2 1.4 scatter_custom_fusion
  12.3 20.5 %all-to-all-start = ((s32[128,4,1]{1,2,0:T(1,128)}), s32[128,4,1]{1,2,0:T(1,128)S(1)}, u32[]{:S(2)}, u32[]{:S(2)}) async-start(s32[128,4,1]{1,2,0:T(1,128)} %bitcast.4), calls=%async_computation | async-start | bytes 131072 | tf_op jit(solution)/shard_map/all_to_all | solution.py:68
  33.9 1.6 fusion.11
  35.4 467.5 %all-reduce.3.cloned.1.call-done = f32[768,768]{0,1:T(8,128)} async-done(((f32[768,768]{0,1:T(8,128)}), f32[768,768]{0,1:T(8,128)}) %all-reduce.3.cloned.1.call-update) | async-done | bytes 2359312 | tf_op jit(solution)/shard_map/psum | solution.py:47
  502.9 3.3 select_add_fusion
  506.3 3.7 copy.39
  510.0 2.0 fusion
  512.0 1.4 copy-done.3
  513.3 11.7 %cholesky.164 = f32[128,128]{1,0:T(8,128)S(1)} custom-call(f32[128,128]{1,0:T(8,128)S(1)} %cholesky.421), custom_call_target="Cholesky" | custom-call | tf_op jit(solution)/shard_map/jit(cholesky)/cholesky | solution.py:48
  525.1 9.8 %custom-call.47 = f32[1,128,128]{1,2,0:T(8,128)S(1)} custom-call(f32[1,128,128]{2,1,0:T(8,128)S(1)} %get-tuple-element.46), custom_call_target="InvertDiagBlocksLowerTriangular" | custom-call | tf_op jit(solution)/shard_map/jit(cholesky)/cholesky | solution.py:48
  534.9 1.4 fusion.33
  536.3 1.4 convolution_subtract_fusion.4
  537.7 11.7 %cholesky.187 = f32[128,128]{1,0:T(8,128)S(1)} custom-call(f32[128,128]{1,0:T(8,128)S(1)} %cholesky.425), custom_call_target="Cholesky" | custom-call | tf_op jit(solution)/shard_map/jit(cholesky)/cholesky | solution.py:48
  550.5 10.6 %custom-call.48 = f32[1,128,128]{1,2,0:T(8,128)} custom-call(f32[1,128,128]{2,1,0:T(8,128)S(1)} %get-tuple-element.44), custom_call_target="InvertDiagBlocksLowerTriangular" | custom-call | tf_op jit(solution)/shard_map/jit(cholesky)/cholesky | solution.py:48
  562.5 1.9 convolution_subtract_fusion.5
  564.5 11.7 %cholesky.352 = f32[128,128]{1,0:T(8,128)S(1)} custom-call(f32[128,128]{1,0:T(8,128)S(1)} %cholesky.430), custom_call_target="Cholesky" | custom-call | tf_op jit(solution)/shard_map/jit(cholesky)/cholesky | solution.py:48
  576.4 9.8 %custom-call.49 = f32[1,128,128]{1,2,0:T(8,128)S(1)} custom-call(f32[1,128,128]{2,1,0:T(8,128)S(1)} %get-tuple-element.42), custom_call_target="InvertDiagBlocksLowerTriangular" | custom-call | tf_op jit(solution)/shard_map/jit(cholesky)/cholesky | solution.py:48
  586.6 2.1 convolution_subtract_fusion.6
  588.7 12.1 %cholesky.371 = f32[128,128]{1,0:T(8,128)S(1)} custom-call(f32[128,128]{1,0:T(8,128)S(1)} %cholesky.435), custom_call_target="Cholesky" | custom-call | tf_op jit(solution)/shard_map/jit(cholesky)/cholesky | solution.py:48
  600.9 9.8 %custom-call.50 = f32[1,128,128]{1,2,0:T(8,128)S(1)} custom-call(f32[1,128,128]{2,1,0:T(8,128)S(1)} %get-tuple-element.40), custom_call_target="InvertDiagBlocksLowerTriangular" | custom-call | tf_op jit(solution)/shard_map/jit(cholesky)/cholesky | solution.py:48
  611.1 1.9 convolution_subtract_fusion.7
  613.0 11.7 %cholesky.390 = f32[128,128]{1,0:T(8,128)S(1)} custom-call(f32[128,128]{1,0:T(8,128)S(1)} %cholesky.440), custom_call_target="Cholesky" | custom-call | tf_op jit(solution)/shard_map/jit(cholesky)/cholesky | solution.py:48
  624.8 9.8 %custom-call.51 = f32[1,128,128]{1,2,0:T(8,128)S(1)} custom-call(f32[1,128,128]{2,1,0:T(8,128)S(1)} %get-tuple-element.38), custom_call_target="InvertDiagBlocksLowerTriangular" | custom-call | tf_op jit(solution)/shard_map/jit(cholesky)/cholesky | solution.py:48
  634.9 1.7 convolution_subtract_fusion.8
  636.7 11.7 %cholesky.408 = f32[128,128]{1,0:T(8,128)S(1)} custom-call(f32[128,128]{1,0:T(8,128)S(1)} %convolution_subtract_fusion.8), custom_call_target="Cholesky" | custom-call | tf_op jit(solution)/shard_map/jit(cholesky)/cholesky | solution.py:48
  655.5 1.6 select_select_fusion
  657.1 21.3 %while.1 = (s32[]{:T(128)}, f32[768,768]{0,1:T(8,128)}, s32[6,2]{0,1:T(2,128)S(1)}, f32[6,128,128]{2,1,0:T(8,128)}, s32[]{:T(128)}) while((s32[]{:T(128)}, f32[768,768]{0,1:T(8,128)}, s32[6,2]{0,1:T(2,128)S(1)}, f32[6,128,128]{2,1,0:T(8,128)}, s32[]{:T(128)}) %tuple.34), condition=%wide.while_cond, body=%wide.while_body.sunk | while | flops 2 | bytes 393829 | solution.py:49
  657.7 2.2 dynamic-slice.7
  661.3 2.2 dynamic-slice.7
  664.9 2.2 dynamic-slice.7
  668.4 2.2 dynamic-slice.7
  672.0 2.2 dynamic-slice.7
  675.5 2.1 dynamic-slice.7
  678.4 59.9 %custom-call.52 = f32[6,128,128]{1,2,0:T(8,128)S(1)} custom-call(f32[6,128,128]{2,1,0:T(8,128)} %get-tuple-element.12), custom_call_target="InvertDiagBlocksLowerTriangular" | custom-call | tf_op jit(solution)/shard_map/jit(_solve_triangular)/triangular_solve | solution.py:49
  739.5 1.8 convolution_subtract_fusion.2
  741.9 2.3 convolution_subtract_fusion.3
  744.8 3.0 convolution_subtract_fusion.1
  748.4 3.6 fusion.12
  752.6 4.6 convolution_subtract_fusion
  758.2 1.5 scatter_custom_fusion.1
  760.5 15.3 %all-to-all-start.1 = ((bf16[128,4,192]{2,1,0:T(4,128)(2,1)}), bf16[128,4,192]{2,1,0:T(4,128)(2,1)S(1)}, u32[]{:S(2)}, u32[]{:S(2)}) async-start(bf16[128,4,192]{2,1,0:T(4,128)(2,1)} %all_to_all.27), calls=%async_computation.1 | async-start | bytes 524288 | tf_op jit(solution)/shard_map/all_to_all | solution.py:67
  777.3 20.9 %all-to-all-done.1 = bf16[128,4,192]{2,1,0:T(4,128)(2,1)S(1)} async-done(((bf16[128,4,192]{2,1,0:T(4,128)(2,1)}), bf16[128,4,192]{2,1,0:T(4,128)(2,1)S(1)}, u32[]{:S(2)}, u32[]{:S(2)}) %all-to-all-start.1) | async-done | bytes 196640 | tf_op jit(solution)/shard_map/all_to_all | solution.py:67
  798.5 11.0 %all_gather.6 = bf16[512,768]{0,1:T(8,128)(2,1)S(1)} all-gather(bf16[512,192]{0,1:T(8,128)(2,1)S(1)} %copy.58), channel_id=1, replica_groups=mesh['dp'=128,'mp'=4] {'mp'}, dimensions={1}, use_global_device_ids=true | all-gather | bytes 983040 | tf_op jit(solution)/shard_map/all_gather | solution.py:70
  810.2 8.2 all-gather
  820.3 11.1 %all-to-all-start.2 = ((f32[128,4,1]{1,2,0:T(1,128)}), f32[128,4,1]{1,2,0:T(1,128)S(1)}, u32[]{:S(2)}, u32[]{:S(2)}) async-start(f32[128,4,1]{1,2,0:T(1,128)} %bitcast.24), calls=%async_computation.2 | async-start | bytes 131072 | tf_op jit(solution)/shard_map/all_to_all | solution.py:77
  831.4 15.1 %all-to-all-done.2 = f32[128,4,1]{1,2,0:T(1,128)S(1)} async-done(((f32[128,4,1]{1,2,0:T(1,128)}), f32[128,4,1]{1,2,0:T(1,128)S(1)}, u32[]{:S(2)}, u32[]{:S(2)}) %all-to-all-start.2) | async-done | bytes 2080 | tf_op jit(solution)/shard_map/all_to_all | solution.py:77
  847.4 2.5 gather_fusion
  (120 shorter events, 29.5 us)
Async XLA Ops:
  6.5 1.0 copy-start
  6.5 496.4 %all-reduce.3.cloned.1.call-start = ((), (), s32[]{:S(2)}) async-start(), calls=%async_computation.3 | async-start | bytes 4718592 | tf_op jit(solution)/shard_map/psum | solution.py:47
  7.5 2.0 copy-start.5
  12.3 748.2 %all-to-all-start = ((s32[128,4,1]{1,2,0:T(1,128)}), s32[128,4,1]{1,2,0:T(1,128)S(1)}, u32[]{:S(2)}, u32[]{:S(2)}) async-start(s32[128,4,1]{1,2,0:T(1,128)} %bitcast.4), calls=%async_computation | async-start | bytes 131072 | tf_op jit(solution)/shard_map/all_to_all | solution.py:68
  506.3 3.7 copy-start.1
  511.9 1.4 copy-start.3
  561.0 1.1 copy-start.4
  678.4 63.5 %copy-start.2 = (f32[768,768]{0,1:T(8,128)S(1)}, f32[768,768]{0,1:T(8,128)}, u32[]{:S(2)}) copy-start(f32[768,768]{0,1:T(8,128)} %fusion.11) | copy-start | bytes 7077892
  760.5 37.7 %all-to-all-start.1 = ((bf16[128,4,192]{2,1,0:T(4,128)(2,1)}), bf16[128,4,192]{2,1,0:T(4,128)(2,1)S(1)}, u32[]{:S(2)}, u32[]{:S(2)}) async-start(bf16[128,4,192]{2,1,0:T(4,128)(2,1)} %all_to_all.27), calls=%async_computation.1 | async-start | bytes 524288 | tf_op jit(solution)/shard_map/all_to_all | solution.py:67
  820.3 26.2 %all-to-all-start.2 = ((f32[128,4,1]{1,2,0:T(1,128)}), f32[128,4,1]{1,2,0:T(1,128)S(1)}, u32[]{:S(2)}, u32[]{:S(2)}) async-start(f32[128,4,1]{1,2,0:T(1,128)} %bitcast.24), calls=%async_computation.2 | async-start | bytes 131072 | tf_op jit(solution)/shard_map/all_to_all | solution.py:77
Sparse Core Ops, SparseCore 0:
  12.6 490.2 all-reduce.2
where the time goes:
time: 862 us; the launch traced here: 857 us
  waiting for transfers between devices  503 us (58%)
  other arithmetic  197 us (23%)
  starting transfers between devices  47 us (5%)
  local copies, waits for them, and re-layouts  39.3 us (5%)
  matrix products  33.7 us (4%)
  blocking collectives  19.1 us (2%)
  between operations  17.9 us (2%)
    psum x1, waiting for transfers between devices, local(): moments = lax.psum(contract_rows(own_rows, own_rows), ('dp', 'mp'))  468 us
    another operation x22, other arithmetic, local(): jnp.linalg.cholesky(moments / float(row_count * dp_count) + 0.001 * ident...  124 us
    another operation x3, other arithmetic, local(): jax.scipy.linalg.solve_triangular(chol_factor, identity, lower=True)  61.5 us
    another operation x33, local copies, waits for them, and re-layouts  21.2 us
    all_to_all x1, waiting for transfers between devices, local(): lax.all_to_all(send_rows, 'dp', split_axis=0, concat_axis=0, tiled=True)  20.9 us
    all_to_all x1, starting transfers between devices, local(): lax.all_to_all(send_ids, 'dp', split_axis=0, concat_axis=0, tiled=True)  20.5 us
    another operation x11, matrix products, local(): jax.scipy.linalg.solve_triangular(chol_factor, identity, lower=True)  19.2 us
  transfers between devices with their start and end apart: 4, of which 3 were waited for; matrix products, arithmetic and copies ran while one was open for 30% of the time, Pallas kernels for 0%

commit v1 on v0

--- a/solution.py
+++ b/solution.py
@@ -44,7 +44,8 @@
     identity = jnp.eye(feat_width, dtype=jnp.float32)
     row_share = row_count // mp_count
     own_rows = lax.dynamic_slice_in_dim(embeddings, mp_index * row_share, row_share, 0)
-    moments = lax.psum(contract_rows(own_rows, own_rows), ("dp", "mp"))
+    inner = lax.psum(contract_rows(own_rows, own_rows), "dp")
+    moments = lax.psum(inner, "mp")
     chol_factor = jnp.linalg.cholesky(moments / float(row_count * dp_count) + 0.001 * identity)
     whitening = jax.scipy.linalg.solve_triangular(chol_factor, identity, lower=True).astype(
         jnp.bfloat16

time: 862 us -> 807 us (0.936)
  waiting for transfers between devices: 503 us -> 455 us
    psum x1 -> x2, waiting for transfers between devices: 468 us -> 419 us  [the longest x1 359 us: local(): inner = lax.psum(contract_rows(own_rows, own_rows), 'dp')]
  transfers between devices with their start and end apart: 4 -> 5, of which waited for: 3 -> 4; matrix products, arithmetic and copies ran while one was open for 30% -> 32% of each run, Pallas kernels for 0% -> 0%
where the time goes in v1:
time: 807 us; the launch traced here: 802 us
  waiting for transfers between devices  455 us (56%)
  other arithmetic  197 us (24%)
  starting transfers between devices  42.8 us (5%)
  local copies, waits for them, and re-layouts  39.3 us (5%)
  matrix products  33.6 us (4%)
  between operations  17.9 us (2%)
  blocking collectives  16.9 us (2%)
    psum x1, waiting for transfers between devices, local(): inner = lax.psum(contract_rows(own_rows, own_rows), 'dp')  359 us
    another operation x22, other arithmetic, local(): jnp.linalg.cholesky(moments / float(row_count * dp_count) + 0.001 * ident...  124 us
    another operation x3, other arithmetic, local(): jax.scipy.linalg.solve_triangular(chol_factor, identity, lower=True)  61.5 us
    psum x1, waiting for transfers between devices, local(): moments = lax.psum(inner, 'mp')  59.8 us
    another operation x33, local copies, waits for them, and re-layouts  21.2 us
    all_to_all x1, waiting for transfers between devices, local(): lax.all_to_all(send_rows, 'dp', split_axis=0, concat_axis=0, tiled=True)  20.9 us
    another operation x11, matrix products, local(): jax.scipy.linalg.solve_triangular(chol_factor, identity, lower=True)  19.2 us
    all_to_all x1, starting transfers between devices, local(): lax.all_to_all(send_rows, 'dp', split_axis=0, concat_axis=0, tiled=True)  16.8 us
  transfers between devices with their start and end apart: 5, of which 4 were waited for; matrix products, arithmetic and copies ran while one was open for 32% of the time, Pallas kernels for 0%

profile of v1, /device:TPU:1, one launch (start us, length us, event | category | flops | bytes accessed | tf_op | source)
XLA Modules:
  0.0 802.1 jit_solution(10875709716127795163)
XLA Ops:
  7.5 1.9 fusion.53
  9.5 359.1 %all-reduce.4.cloned.1.call-done = f32[768,768]{0,1:T(8,128)} async-done(((f32[768,768]{0,1:T(8,128)}), f32[768,768]{0,1:T(8,128)}) %all-reduce.4.cloned.1.call-update) | async-done | bytes 2359312 | tf_op jit(solution)/shard_map/psum | solution.py:47
  369.3 1.4 scatter_custom_fusion
  371.5 13.6 %all-to-all-start = ((s32[128,4,1]{1,2,0:T(1,128)}), s32[128,4,1]{1,2,0:T(1,128)S(1)}, u32[]{:S(2)}, u32[]{:S(2)}) async-start(s32[128,4,1]{1,2,0:T(1,128)} %bitcast.4), calls=%async_computation | async-start | bytes 131072 | tf_op jit(solution)/shard_map/all_to_all | solution.py:69
  386.1 1.6 fusion.11
  387.6 59.8 %all-reduce.6.cloned.1.call-done = f32[768,768]{0,1:T(8,128)} async-done(((f32[768,768]{0,1:T(8,128)}), f32[768,768]{0,1:T(8,128)}) %all-reduce.6.cloned.1.call-update) | async-done | bytes 2359312 | tf_op jit(solution)/shard_map/psum | solution.py:48
  447.5 3.3 select_add_fusion
  450.8 3.7 copy.39
  454.5 2.0 fusion
  457.9 11.7 %cholesky.164 = f32[128,128]{1,0:T(8,128)S(1)} custom-call(f32[128,128]{1,0:T(8,128)S(1)} %cholesky.421), custom_call_target="Cholesky" | custom-call | tf_op jit(solution)/shard_map/jit(cholesky)/cholesky | solution.py:49
  469.6 9.8 %custom-call.47 = f32[1,128,128]{1,2,0:T(8,128)S(1)} custom-call(f32[1,128,128]{2,1,0:T(8,128)S(1)} %get-tuple-element.46), custom_call_target="InvertDiagBlocksLowerTriangular" | custom-call | tf_op jit(solution)/shard_map/jit(cholesky)/cholesky | solution.py:49
  479.4 1.4 fusion.33
  480.8 1.4 convolution_subtract_fusion.4
  482.3 11.7 %cholesky.187 = f32[128,128]{1,0:T(8,128)S(1)} custom-call(f32[128,128]{1,0:T(8,128)S(1)} %cholesky.425), custom_call_target="Cholesky" | custom-call | tf_op jit(solution)/shard_map/jit(cholesky)/cholesky | solution.py:49
  495.0 10.6 %custom-call.48 = f32[1,128,128]{1,2,0:T(8,128)} custom-call(f32[1,128,128]{2,1,0:T(8,128)S(1)} %get-tuple-element.44), custom_call_target="InvertDiagBlocksLowerTriangular" | custom-call | tf_op jit(solution)/shard_map/jit(cholesky)/cholesky | solution.py:49
  507.1 1.9 convolution_subtract_fusion.5
  509.0 11.7 %cholesky.352 = f32[128,128]{1,0:T(8,128)S(1)} custom-call(f32[128,128]{1,0:T(8,128)S(1)} %cholesky.430), custom_call_target="Cholesky" | custom-call | tf_op jit(solution)/shard_map/jit(cholesky)/cholesky | solution.py:49
  520.9 9.8 %custom-call.49 = f32[1,128,128]{1,2,0:T(8,128)S(1)} custom-call(f32[1,128,128]{2,1,0:T(8,128)S(1)} %get-tuple-element.42), custom_call_target="InvertDiagBlocksLowerTriangular" | custom-call | tf_op jit(solution)/shard_map/jit(cholesky)/cholesky | solution.py:49
  531.1 2.1 convolution_subtract_fusion.6
  533.2 12.1 %cholesky.371 = f32[128,128]{1,0:T(8,128)S(1)} custom-call(f32[128,128]{1,0:T(8,128)S(1)} %cholesky.435), custom_call_target="Cholesky" | custom-call | tf_op jit(solution)/shard_map/jit(cholesky)/cholesky | solution.py:49
  545.5 9.8 %custom-call.50 = f32[1,128,128]{1,2,0:T(8,128)S(1)} custom-call(f32[1,128,128]{2,1,0:T(8,128)S(1)} %get-tuple-element.40), custom_call_target="InvertDiagBlocksLowerTriangular" | custom-call | tf_op jit(solution)/shard_map/jit(cholesky)/cholesky | solution.py:49
  555.6 1.9 convolution_subtract_fusion.7
  557.5 11.7 %cholesky.390 = f32[128,128]{1,0:T(8,128)S(1)} custom-call(f32[128,128]{1,0:T(8,128)S(1)} %cholesky.440), custom_call_target="Cholesky" | custom-call | tf_op jit(solution)/shard_map/jit(cholesky)/cholesky | solution.py:49
  569.4 9.8 %custom-call.51 = f32[1,128,128]{1,2,0:T(8,128)S(1)} custom-call(f32[1,128,128]{2,1,0:T(8,128)S(1)} %get-tuple-element.38), custom_call_target="InvertDiagBlocksLowerTriangular" | custom-call | tf_op jit(solution)/shard_map/jit(cholesky)/cholesky | solution.py:49
  579.5 1.7 convolution_subtract_fusion.8
  581.2 11.7 %cholesky.408 = f32[128,128]{1,0:T(8,128)S(1)} custom-call(f32[128,128]{1,0:T(8,128)S(1)} %convolution_subtract_fusion.8), custom_call_target="Cholesky" | custom-call | tf_op jit(solution)/shard_map/jit(cholesky)/cholesky | solution.py:49
  600.1 1.6 select_select_fusion
  601.6 21.3 %while.1 = (s32[]{:T(128)}, f32[768,768]{0,1:T(8,128)}, s32[6,2]{0,1:T(2,128)S(1)}, f32[6,128,128]{2,1,0:T(8,128)}, s32[]{:T(128)}) while((s32[]{:T(128)}, f32[768,768]{0,1:T(8,128)}, s32[6,2]{0,1:T(2,128)S(1)}, f32[6,128,128]{2,1,0:T(8,128)}, s32[]{:T(128)}) %tuple.34), condition=%wide.while_cond, body=%wide.while_body.sunk | while | flops 2 | bytes 393829 | solution.py:50
  602.3 2.2 dynamic-slice.7
  605.8 2.2 dynamic-slice.7
  609.4 2.2 dynamic-slice.7
  613.0 2.2 dynamic-slice.7
  616.5 2.2 dynamic-slice.7
  620.1 2.1 dynamic-slice.7
  622.9 59.9 %custom-call.52 = f32[6,128,128]{1,2,0:T(8,128)S(1)} custom-call(f32[6,128,128]{2,1,0:T(8,128)} %get-tuple-element.12), custom_call_target="InvertDiagBlocksLowerTriangular" | custom-call | tf_op jit(solution)/shard_map/jit(_solve_triangular)/triangular_solve | solution.py:50
  684.1 1.8 convolution_subtract_fusion.2
  686.4 2.3 convolution_subtract_fusion.3
  689.3 3.0 convolution_subtract_fusion.1
  693.0 3.6 fusion.12
  697.2 4.6 convolution_subtract_fusion
  702.7 1.5 scatter_custom_fusion.1
  705.0 16.8 %all-to-all-start.1 = ((bf16[128,4,192]{2,1,0:T(4,128)(2,1)}), bf16[128,4,192]{2,1,0:T(4,128)(2,1)S(1)}, u32[]{:S(2)}, u32[]{:S(2)}) async-start(bf16[128,4,192]{2,1,0:T(4,128)(2,1)} %all_to_all.27), calls=%async_computation.1 | async-start | bytes 524288 | tf_op jit(solution)/shard_map/all_to_all | solution.py:68
  723.4 20.9 %all-to-all-done.1 = bf16[128,4,192]{2,1,0:T(4,128)(2,1)S(1)} async-done(((bf16[128,4,192]{2,1,0:T(4,128)(2,1)}), bf16[128,4,192]{2,1,0:T(4,128)(2,1)S(1)}, u32[]{:S(2)}, u32[]{:S(2)}) %all-to-all-start.1) | async-done | bytes 196640 | tf_op jit(solution)/shard_map/all_to_all | solution.py:68
  744.5 11.7 %all_gather.6 = bf16[512,768]{0,1:T(8,128)(2,1)S(1)} all-gather(bf16[512,192]{0,1:T(8,128)(2,1)S(1)} %copy.58), channel_id=1, replica_groups=mesh['dp'=128,'mp'=4] {'mp'}, dimensions={1}, use_global_device_ids=true | all-gather | bytes 983040 | tf_op jit(solution)/shard_map/all_gather | solution.py:71
  757.0 5.2 all-gather
  764.2 12.3 %all-to-all-start.2 = ((f32[128,4,1]{1,2,0:T(1,128)}), f32[128,4,1]{1,2,0:T(1,128)S(1)}, u32[]{:S(2)}, u32[]{:S(2)}) async-start(f32[128,4,1]{1,2,0:T(1,128)} %bitcast.24), calls=%async_computation.2 | async-start | bytes 131072 | tf_op jit(solution)/shard_map/all_to_all | solution.py:78
  776.5 15.1 %all-to-all-done.2 = f32[128,4,1]{1,2,0:T(1,128)S(1)} async-done(((f32[128,4,1]{1,2,0:T(1,128)}), f32[128,4,1]{1,2,0:T(1,128)S(1)}, u32[]{:S(2)}, u32[]{:S(2)}) %all-to-all-start.2) | async-done | bytes 2080 | tf_op jit(solution)/shard_map/all_to_all | solution.py:78
  792.5 2.5 gather_fusion
  (123 shorter events, 30.9 us)
Async XLA Ops:
  6.5 1.0 copy-start
  6.5 362.1 %all-reduce.4.cloned.1.call-start = ((), (), s32[]{:S(2)}) async-start(), calls=%async_computation.3 | async-start | bytes 4718592 | tf_op jit(solution)/shard_map/psum | solution.py:47
  9.5 359.2 %copy-start.5 = (s32[256]{0:T(256)S(1)}, s32[256]{0:T(256)}, u32[]{:S(2)}) copy-start(s32[256]{0:T(256)} %param.3) | copy-start | bytes 3076
  9.5 438.0 %all-reduce.6.cloned.1.call-start = ((), (), s32[]{:S(2)}) async-start(), calls=%async_computation.4 | async-start | bytes 4718592 | tf_op jit(solution)/shard_map/psum | solution.py:48
  371.5 333.6 %all-to-all-start = ((s32[128,4,1]{1,2,0:T(1,128)}), s32[128,4,1]{1,2,0:T(1,128)S(1)}, u32[]{:S(2)}, u32[]{:S(2)}) async-start(s32[128,4,1]{1,2,0:T(1,128)} %bitcast.4), calls=%async_computation | async-start | bytes 131072 | tf_op jit(solution)/shard_map/all_to_all | solution.py:69
  450.8 3.7 copy-start.1
  456.5 1.4 copy-start.3
  505.6 1.1 copy-start.4
  622.9 63.5 %copy-start.2 = (f32[768,768]{0,1:T(8,128)S(1)}, f32[768,768]{0,1:T(8,128)}, u32[]{:S(2)}) copy-start(f32[768,768]{0,1:T(8,128)} %fusion.11) | copy-start | bytes 7077892
  705.0 39.2 %all-to-all-start.1 = ((bf16[128,4,192]{2,1,0:T(4,128)(2,1)}), bf16[128,4,192]{2,1,0:T(4,128)(2,1)S(1)}, u32[]{:S(2)}, u32[]{:S(2)}) async-start(bf16[128,4,192]{2,1,0:T(4,128)(2,1)} %all_to_all.27), calls=%async_computation.1 | async-start | bytes 524288 | tf_op jit(solution)/shard_map/all_to_all | solution.py:68
  764.2 27.4 %all-to-all-start.2 = ((f32[128,4,1]{1,2,0:T(1,128)}), f32[128,4,1]{1,2,0:T(1,128)S(1)}, u32[]{:S(2)}, u32[]{:S(2)}) async-start(f32[128,4,1]{1,2,0:T(1,128)} %bitcast.24), calls=%async_computation.2 | async-start | bytes 131072 | tf_op jit(solution)/shard_map/all_to_all | solution.py:78
Sparse Core Ops, SparseCore 0:
  10.7 357.8 all-reduce.3
  371.0 76.4 all-reduce.5
